TPU v7x, 32 devices: a whole 2x2x4 slice. The times are simulated.
32 devices in a mesh: node: 2 (over y), sub: 16 (over z, x, core).
Axes of the slice: x: 2, y: 2, z: 4, core: 2. Of those that a mesh axis runs over, the one named last changes fastest.
Arguments:
- inner_inverse: bfloat16 [2, 16, 2, 1024, 1024], P('node', 'sub'), may hold values from -1 to 2
- schur_inverse: bfloat16 [2, 2, 2048, 2048], P('node', None, 'sub'), may hold values from -1 to 2
- coupling: bfloat16 [16, 1024, 128], P('sub'), may hold values from -0.5 to 0.5
- iface_index: int32 [16, 128], P('sub'), may hold values from 0 to 2047, as said below
- basis_inner: bfloat16 [16384, 384], P('sub'), may hold values from -2134 to 2134
- basis_iface: bfloat16 [2048, 384], P('sub'), may hold values from -134 to 134
- node_weights: float32 [2, 2], P('node'), may hold values from -4 to 4
Outputs:
- filtered_inner: float32 [16384, 384], P('sub')
- filtered_iface: float32 [2048, 384], P('sub')
Inputs may be any that keep to these rules, and one draw needn't show every extreme that they name: `iface_index`: over all rows every interface unknown from 0 to 2047 appears exactly once.
All inputs are finite; a program needn't handle non-finite values.
Results may differ from a plain program's by a relative error of at most 0.0086.
Values may be sent and summed in bfloat16 or wider, within the bound.
A program may use at most 64 MiB of HBM per device.

v0:
```python
import jax
import jax.numpy as jnp
from jax import lax
from jax.sharding import PartitionSpec as P


def gram_part(first_rows, second_rows):
    first_gram = jnp.einsum("rm,rn->mn", first_rows, first_rows, precision=lax.Precision.HIGHEST)
    return first_gram + jnp.einsum(
        "rm,rn->mn", second_rows, second_rows, precision=lax.Precision.HIGHEST
    )


def cholesky_apply(gram_matrix, first_rows, second_rows):
    lower_factor = jnp.linalg.cholesky(gram_matrix)
    first_out = lax.linalg.triangular_solve(
        lower_factor, first_rows, left_side=False, lower=True, transpose_a=True
    )
    second_out = lax.linalg.triangular_solve(
        lower_factor, second_rows, left_side=False, lower=True, transpose_a=True
    )
    return (first_out, second_out)


def complex_rows(part_real, part_imag, block_piece, columns):
    from_real = jnp.dot(part_real, block_piece, preferred_element_type=jnp.float32)
    from_imag = jnp.dot(part_imag, block_piece, preferred_element_type=jnp.float32)
    return jnp.concatenate(
        [
            from_real[:, :columns] - from_imag[:, columns:],
            from_real[:, columns:] + from_imag[:, :columns],
        ],
        axis=1,
    )


def per_device(
    inner_inverse, schur_inverse, coupling, iface_index, basis_inner, basis_iface, node_weights
):
    inner_rows = basis_inner.shape[0]
    columns = basis_inner.shape[1]
    iface_rows = basis_iface.shape[0]
    stacked_inverse = inner_inverse[0, 0].reshape(2 * inner_rows, inner_rows)
    couple_block = coupling[0]
    index_row = iface_index[0]
    inner_solve = jnp.dot(stacked_inverse, basis_inner, preferred_element_type=jnp.float32).astype(
        jnp.bfloat16
    )
    iface_contrib = jnp.einsum(
        "il,cim->lcm",
        couple_block,
        inner_solve.reshape(2, inner_rows, columns),
        preferred_element_type=jnp.float32,
    )
    iface_contrib = iface_contrib.astype(jnp.bfloat16).reshape(iface_rows, 2 * columns)
    schur_real = schur_inverse[0, 0]
    schur_imag = schur_inverse[0, 1]
    all_contrib, all_basis, all_index = (
        lax.all_gather(iface_contrib, "sub", axis=0, tiled=True),
        lax.all_gather(basis_iface, "sub", axis=0, tiled=True),
        lax.all_gather(iface_index, "sub", axis=0, tiled=True),
    )
    flat_index = all_index.reshape(-1).astype(jnp.int32)
    total_rows = flat_index.shape[0]
    inverse_order = (
        jnp.zeros((total_rows,), jnp.int32)
        .at[flat_index]
        .set(jnp.arange(total_rows, dtype=jnp.int32))
    )
    arranged = jnp.take(all_contrib, inverse_order, axis=0).astype(jnp.float32)
    full_right = jnp.concatenate(
        [all_basis.astype(jnp.float32) - arranged[:, :columns], -arranged[:, columns:]], axis=1
    ).astype(jnp.bfloat16)
    solved = complex_rows(schur_real, schur_imag, full_right, columns)
    iface_solution = solved.astype(jnp.bfloat16)
    block_piece = lax.all_gather(iface_solution, "sub", axis=0, tiled=True)
    width_rows = block_piece.shape[0]
    targets = lax.broadcasted_iota(jnp.int32, (iface_rows, width_rows), 1)
    selector = (targets == index_row[:, None]).astype(jnp.bfloat16)
    picked = jnp.dot(selector, block_piece, preferred_element_type=jnp.float32).astype(jnp.bfloat16)
    correction = jnp.dot(couple_block, picked, preferred_element_type=jnp.float32).astype(
        jnp.bfloat16
    )
    inner_fix = jnp.dot(stacked_inverse, correction, preferred_element_type=jnp.float32)
    fix_real = inner_fix[:inner_rows, :columns] - inner_fix[inner_rows:, columns:]
    fix_imag = inner_fix[:inner_rows, columns:] + inner_fix[inner_rows:, :columns]
    full_real = inner_solve[:inner_rows].astype(jnp.float32) - fix_real
    full_imag = inner_solve[inner_rows:].astype(jnp.float32) - fix_imag
    weight_real = node_weights[0, 0]
    weight_imag = node_weights[0, 1]
    term_inner = weight_real * full_real - weight_imag * full_imag
    solution_wide = iface_solution.astype(jnp.float32)
    term_iface = weight_real * solution_wide[:, :columns] - weight_imag * solution_wide[:, columns:]
    row_total = lax.axis_size("sub") * (inner_rows + iface_rows)
    filt_inner, filt_iface = lax.psum((term_inner, term_iface), "node")
    gram_matrix = lax.psum(gram_part(filt_inner, filt_iface), "sub")
    filtered_inner, filtered_iface = cholesky_apply(gram_matrix / row_total, filt_inner, filt_iface)
    return (filtered_inner, filtered_iface)


def solution(mesh):
    return jax.shard_map(
        per_device,
        mesh=mesh,
        in_specs=(
            P("node", "sub", None, None, None),
            P("node", None, "sub", None),
            P("sub", None, None),
            P("sub", None),
            P("sub", None),
            P("sub", None),
            P("node", None),
        ),
        out_specs=(P("sub", None), P("sub", None)),
        check_vma=False,
    )
```

profile of v0, /device:TPU:0, one launch (start us, length us, event | category | flops | bytes accessed | tf_op | source)
XLA Modules:
  0.0 455.9 jit_solution(13545626614218891070)
XLA Ops:
  8.3 4.6 %convolution_convert_fusion = bf16[2048,384]{1,0:T(8,128)(2,1)S(1)} fusion(bf16[2048,1024]{1,0:T(8,128)(2,1)} %bitcast.91, bf16[1024,384]{1,0:T(8,128)(2,1)S(1)} %copy-done), kind=kOutput, calls=%fused_computation.11 | convolution fusion | flops 1611399168 | bytes 6553600 | tf_op jit(solution)/shard_map/dot_general | solution.py:46
  15.2 23.1 %all-gather = s32[16,1,128]{2,1,0:T(1,128)S(1)} all-gather(s32[1,1,128]{2,1,0:T(1,128)S(1)} %bitcast.89), channel_id=1, replica_groups=mesh['node'=2,'sub'=16] {'sub'}, dimensions={0}, use_global_device_ids=true | all-gather | bytes 8704 | tf_op jit(solution)/shard_map/all_gather | solution.py:61
  38.3 8.0 %scatter_custom_fusion = s32[2048]{0:T(1024)S(1)} fusion(s32[2048]{0:T(1024)S(1)} %bitcast.88, s32[2048]{0:T(1024)S(1)} %iota.70, s32[]{:T(128)} %copy.44), kind=kCustom, calls=%fused_computation.96 | custom fusion | bytes 8196 | tf_op jit(solution)/shard_map/scatter | solution.py:68
  46.4 16.3 %all-gather.7.cloned.1.call-done = bf16[2048,768]{1,0:T(8,128)(2,1)} async-done(((bf16[128,768]{1,0:T(8,128)(2,1)}), bf16[2048,768]{1,0:T(8,128)(2,1)}) %all-gather.7.cloned.1.call-update) | async-done | bytes 3145744 | tf_op jit(solution)/shard_map/all_gather | solution.py:59
  62.8 12.4 %gather_fusion = bf16[2048,768]{1,0:T(8,128)(2,1)} fusion(bf16[2048,768]{1,0:T(8,128)(2,1)} %all-gather.7.cloned.1.call-done, s32[2048]{0:T(1024)S(1)} %fusion.48), kind=kCustom, calls=%fused_computation | custom fusion | bytes 6299648 | tf_op jit(solution)/shard_map/jit(_take)/gather | solution.py:70
  75.2 4.3 select_convert_fusion
  79.5 23.5 %all-gather.5.cloned.1.call-done = bf16[2048,384]{1,0:T(8,128)(2,1)} async-done(((bf16[128,384]{1,0:T(8,128)(2,1)}), bf16[2048,384]{1,0:T(8,128)(2,1)}) %all-gather.5.cloned.1.call-update) | async-done | bytes 1572880 | tf_op jit(solution)/shard_map/all_gather | solution.py:60
  103.0 3.9 fusion.1
  110.9 2.0 fusion.25
  112.9 42.1 %all-gather.9.cloned.1.call-done = bf16[2048,768]{0,1:T(8,128)(2,1)} async-done(((bf16[128,768]{0,1:T(8,128)(2,1)}), bf16[2048,768]{0,1:T(8,128)(2,1)}) %all-gather.9.cloned.1.call-update) | async-done | bytes 3145744 | tf_op jit(solution)/shard_map/all_gather | solution.py:76
  155.0 3.1 convolution_convert_fusion.2
  158.0 8.7 %convolution_bitcast_fusion = f32[2048,768]{1,0:T(8,128)} fusion(bf16[2048,1024]{1,0:T(8,128)(2,1)} %bitcast.92, bf16[128,768]{1,0:T(8,128)(2,1)S(1)} %convolution_convert_fusion.2, bf16[1,1024,128]{2,1,0:T(8,128)(2,1)S(1)} %copy-done.8), kind=kOutput, calls=%fused_computation.4 | convolution fusion | flops 3423338496 | bytes 10944512 | tf_op jit(solution)/shard_map/dot_general | solution.py:84
  166.7 5.7 %fusion.6 = f32[1024,384]{1,0:T(8,128)} fusion(f32[2048,768]{1,0:T(8,128)} %convolution_bitcast_fusion, bf16[2048,384]{1,0:T(8,128)(2,1)S(1)} %convolution_convert_fusion, f32[]{:T(128)} %bitcast.16, f32[]{:T(128)} %bitcast), kind=kLoop, calls=%fused_computation.18 | loop fusion | flops 3538944 | bytes 9437192 | tf_op jit(solution)/shard_map/sub | solution.py:91
  172.5 54.1 %all-reduce.7.cloned.1.call-done = (f32[1024,384]{1,0:T(8,128)}, f32[128,384]{0,1:T(8,128)}) async-done(((f32[1024,384]{1,0:T(8,128)}, f32[128,384]{0,1:T(8,128)}), (f32[1024,384]{1,0:T(8,128)}, f32[128,384]{0,1:T(8,128)})) %all-reduce.7.cloned.1.call-update) | async-done | bytes 1769488 | tf_op jit(solution)/shard_map/psum | solution.py:95
  226.6 4.7 %fusion.58 = f32[384,384]{0,1:T(8,128)S(1)} fusion(f32[1024,384]{1,0:T(8,128)} %get-tuple-element.22), kind=kOutput, calls=%fused_computation.112 | convolution fusion | flops 1811939328 | bytes 2162688 | tf_op jit(solution)/shard_map/rm,rn->mn/dot_general | solution.py:8
  231.3 1.5 convolution_add_fusion
  232.8 92.1 %all-reduce.5.cloned.1.call-done = f32[384,384]{0,1:T(8,128)} async-done(((f32[384,384]{0,1:T(8,128)}), f32[384,384]{0,1:T(8,128)}) %all-reduce.5.cloned.1.call-update) | async-done | bytes 589840 | tf_op jit(solution)/shard_map/psum | solution.py:96
  326.4 11.7 %cholesky.77 = f32[128,128]{1,0:T(8,128)S(1)} custom-call(f32[128,128]{1,0:T(8,128)S(1)} %cholesky.192), custom_call_target="Cholesky" | custom-call | tf_op jit(solution)/shard_map/jit(cholesky)/cholesky | solution.py:15
  338.2 9.8 %custom-call.24 = f32[1,128,128]{1,2,0:T(8,128)S(1)} custom-call(f32[1,128,128]{2,1,0:T(8,128)S(1)} %get-tuple-element.38), custom_call_target="InvertDiagBlocksLowerTriangular" | custom-call | tf_op jit(solution)/shard_map/jit(cholesky)/cholesky | solution.py:15
  349.9 13.3 %cholesky.162 = f32[128,128]{1,0:T(8,128)} custom-call(f32[128,128]{1,0:T(8,128)} %cholesky.196), custom_call_target="Cholesky" | custom-call | tf_op jit(solution)/shard_map/jit(cholesky)/cholesky | solution.py:15
  363.2 1.5 select_reduce_fusion.1
  364.7 11.3 %custom-call.25 = f32[1,128,128]{1,2,0:T(8,128)} custom-call(f32[1,128,128]{2,1,0:T(8,128)} %get-tuple-element.35), custom_call_target="InvertDiagBlocksLowerTriangular" | custom-call | tf_op jit(solution)/shard_map/jit(cholesky)/cholesky | solution.py:15
  378.0 12.5 %cholesky.181 = f32[128,128]{1,0:T(8,128)S(1)} custom-call(f32[128,128]{1,0:T(8,128)} %convolution_subtract_fusion.5), custom_call_target="Cholesky" | custom-call | tf_op jit(solution)/shard_map/jit(cholesky)/cholesky | solution.py:15
  394.9 7.8 %while.1 = (s32[]{:T(128)}, f32[384,384]{1,0:T(8,128)S(1)}, s32[3,2]{0,1:T(2,128)S(1)}, f32[3,128,128]{2,1,0:T(8,128)}, s32[]{:T(128)}) while((s32[]{:T(128)}, f32[384,384]{1,0:T(8,128)S(1)}, s32[3,2]{0,1:T(2,128)S(1)}, f32[3,128,128]{2,1,0:T(8,128)}, s32[]{:T(128)}) %tuple.35), condition=%wide.while_cond, body=%wide.while_body.sunk | while | flops 2 | bytes 132705 | solution.py:16
  395.8 1.9 bitcast_dynamic-update-slice_fusion.2
  398.3 1.9 bitcast_dynamic-update-slice_fusion.2
  400.8 1.9 bitcast_dynamic-update-slice_fusion.2
  402.8 30.3 %custom-call.26 = f32[3,128,128]{1,2,0:T(8,128)S(1)} custom-call(f32[3,128,128]{2,1,0:T(8,128)} %get-tuple-element.9), custom_call_target="InvertDiagBlocksLowerTriangular" | custom-call | tf_op jit(solution)/shard_map/triangular_solve | solution.py:16
  434.9 1.5 fusion.15
  441.5 1.7 copy.24
  444.9 1.8 convolution_subtract_fusion
  447.5 1.6 copy.23
  (79 shorter events, 26.4 us)
Async XLA Ops:
  7.2 1.1 copy-start
  7.2 55.6 %all-gather.7.cloned.1.call-start = ((), (), s32[]{:S(2)}) async-start(), calls=%async_computation.1 | async-start | bytes 3342336 | tf_op jit(solution)/shard_map/all_gather | solution.py:59
  8.3 4.6 %copy-start.8 = (bf16[1,1024,128]{2,1,0:T(8,128)(2,1)S(1)}, bf16[1,1024,128]{2,1,0:T(8,128)(2,1)}, u32[]{:S(2)}) copy-start(bf16[1,1024,128]{2,1,0:T(8,128)(2,1)} %param.9) | copy-start | bytes 786436
  12.9 2.3 copy-start.10
  14.4 88.6 %all-gather.5.cloned.1.call-start = ((), (), s32[]{:S(2)}) async-start(), calls=%async_computation | async-start | bytes 1671168 | tf_op jit(solution)/shard_map/all_gather | solution.py:60
  15.1 139.8 %all-gather.9.cloned.1.call-start = ((), (), s32[]{:S(2)}) async-start(), calls=%async_computation.2 | async-start | bytes 3342336 | tf_op jit(solution)/shard_map/all_gather | solution.py:76
  103.0 3.9 copy-start.11
  109.0 1.3 copy-start.9
  109.8 116.8 %all-reduce.7.cloned.1.call-start = ((), (), s32[]{:S(2)}) async-start(), calls=%async_computation.4 | async-start | bytes 3538944 | tf_op jit(solution)/shard_map/psum | solution.py:95
  172.5 152.4 %all-reduce.5.cloned.1.call-start = ((), (), s32[]{:S(2)}) async-start(), calls=%async_computation.3 | async-start | bytes 1179648 | tf_op jit(solution)/shard_map/psum | solution.py:96
  226.6 4.7 %copy-start.4 = (f32[128,384]{0,1:T(8,128)S(1)}, f32[128,384]{0,1:T(8,128)}, u32[]{:S(2)}) copy-start(f32[128,384]{0,1:T(8,128)} %get-tuple-element.23) | copy-start | bytes 589828
  324.9 1.4 copy-start.3
  348.6 0.7 copy-start.7
  349.2 85.7 %copy-start.1 = (f32[1024,384]{1,0:T(8,128)S(1)}, f32[1024,384]{1,0:T(8,128)}, u32[]{:S(2)}) copy-start(f32[1024,384]{1,0:T(8,128)} %get-tuple-element.22) | copy-start | bytes 4718596
  390.5 3.3 copy-start.2
  433.1 0.7 copy-start.5
  443.3 1.0 copy-start.6
Sparse Core Ops, SparseCore 0:
  14.5 48.2 all-gather.6
  65.0 37.9 all-gather.4
  109.9 45.0 all-gather.8
  172.6 53.9 all-reduce.6
  232.9 91.9 all-reduce.4
where the time goes:
time: 463 us; the launch traced here: 456 us
  waiting for transfers between devices  229 us (49%)
  other arithmetic  112 us (24%)
  matrix products  38.7 us (8%)
  local copies, waits for them, and re-layouts  36.2 us (8%)
  blocking collectives  23.1 us (5%)
  between operations  16.2 us (3%)
    psum x1, waiting for transfers between devices, per_device(): gram_matrix = lax.psum(gram_part(filt_inner, filt_iface), 'sub')  92.1 us
    another operation x10, other arithmetic, cholesky_apply(): lower_factor = jnp.linalg.cholesky(gram_matrix)  61.6 us
    psum x1, waiting for transfers between devices, per_device(): filt_inner, filt_iface = lax.psum((term_inner, term_iface), 'node')  54.1 us
    all_gather x1, waiting for transfers between devices, per_device(): block_piece = lax.all_gather(iface_solution, 'sub', axis=0, tiled=True)  42.1 us
    another operation x4, other arithmetic, cholesky_apply(): lax.linalg.triangular_solve(lower_factor, first_rows, left_side=False, lo...  31.6 us
    all_gather x1, waiting for transfers between devices, per_device(): lax.all_gather(basis_iface, 'sub', axis=0, tiled=True)  23.5 us
    all_gather x1, blocking collectives, per_device(): lax.all_gather(iface_index, 'sub', axis=0, tiled=True)  23.1 us
    all_gather x1, waiting for transfers between devices, per_device(): lax.all_gather(iface_contrib, 'sub', axis=0, tiled=True)  16.3 us
  transfers between devices with their start and end apart: 5, of which 5 were waited for; matrix products, arithmetic and copies ran while one was open for 6% of the time, Pallas kernels for 0%

commit v1 on v0

v1 whole, which is shorter than its diff:
```python
import functools
import jax
import jax.numpy as jnp
from jax import lax
from jax.experimental import pallas as pl
from jax.experimental.pallas import tpu as pltpu
from jax.sharding import PartitionSpec as P

MESH = pl.DeviceIdType.MESH
LANE = 128
F32 = jnp.float32
BF16 = jnp.bfloat16
TN = (((0,), (0,)), ((), ()))
NT = (((1,), (1,)), ((), ()))


class Gather:
    def __init__(self, na, nb, buf, send, recv):
        self.na, self.nb, self.buf, self.send, self.recv = na, nb, buf, send, recv
        node = lax.axis_index("node")
        me = lax.axis_index("sub")
        self.a = me // (2 * nb)
        self.b = (me // 2) % nb
        self.c = me % 2
        self.node = node
        self.me = me

    def slot(self, a, b, c):
        return (a * self.nb + b) * 2 + c

    def copy(self, origin, kind, place, target):
        return pltpu.make_async_remote_copy(
            src_ref=self.buf.at[origin],
            dst_ref=self.buf.at[origin],
            send_sem=self.send.at[kind, place],
            recv_sem=self.recv.at[origin],
            device_id=(self.node, target),
            device_id_type=MESH,
        )

    def routes(self, oa, ob):
        a, b = self.a, self.b
        return (
            (0, (ob == b) & (oa <= a) & (a + 1 < self.na), self.slot(a + 1, b, self.c)),
            (1, (ob == b) & (oa >= a) & (a >= 1), self.slot(a - 1, b, self.c)),
            (2, (ob <= b) & (b + 1 < self.nb), self.slot(a, b + 1, self.c)),
            (3, (ob >= b) & (b >= 1), self.slot(a, b - 1, self.c)),
        )

    def handle(self, oa, ob, own):
        origin = self.slot(oa, ob, self.c)
        place = oa * self.nb + ob
        sibling = self.slot(self.a, self.b, 1 - self.c)
        if not own:
            self.copy(origin, 4, place, sibling).wait_recv()
        for kind, cond, target in self.routes(oa, ob):

            @pl.when(cond)
            def _(kind=kind, target=target):
                self.copy(origin, kind, place, target).start()

        self.copy(origin, 4, place, sibling).start()

    def step(self, tau):
        if tau == 0:
            self.handle(self.a, self.b, True)
            return
        for tb in range(self.nb):
            t = tau - tb
            if t < 0 or t >= self.na:
                continue
            for sa in (-1, 1) if t else (1,):
                for sb in (-1, 1) if tb else (1,):
                    oa, ob = self.a + sa * t, self.b + sb * tb
                    ok = (oa >= 0) & (oa < self.na) & (ob >= 0) & (ob < self.nb)

                    @pl.when(ok)
                    def _(oa=oa, ob=ob):
                        self.handle(oa, ob, False)

    @property
    def steps(self):
        return self.na + self.nb - 1

    def finish(self):
        sibling = self.slot(self.a, self.b, 1 - self.c)

        @pl.loop(0, self.na * self.nb)
        def _(place):
            oa, ob = place // self.nb, place % self.nb
            self.copy(place * 2 + 1 - self.c, 4, place, sibling).wait_recv()
            for kind, cond, target in self.routes(oa, ob):

                @pl.when(cond)
                def _(kind=kind, target=target):
                    self.copy(place * 2 + self.c, kind, place, target).wait_send()

            self.copy(place * 2 + self.c, 4, place, sibling).wait_send()


def step_kernel(
    dims, inv_hbm, schur_hbm, couple, index, basis_in, basis_if, weights,
    filt, gbuf,
    inv, schur, solve, idx_all, bas_all, con_all, sol_all, sperm, work, term, tsend, trecv, g6, grecv, nrecv,
    ld, isend, irecv, bsend, brecv, csend, crecv, ssend, srecv, tss, trs, fss, frs, gss, grs, nss, nrs, ass_, ars,
):
    na, nb, nodes = dims
    subs = na * nb * 2
    ni = inv.shape[1]
    m = basis_in.shape[1]
    lg = couple.shape[1]
    total = schur.shape[2]
    rows = ni + lg
    ch = rows // nodes
    node = lax.axis_index("node")
    me = lax.axis_index("sub")

    load_inv = pltpu.make_async_copy(inv_hbm, inv, ld.at[0])
    load_schur = pltpu.make_async_copy(schur_hbm, schur, ld.at[1])
    put_idx = pltpu.make_async_copy(index, idx_all.at[me], ld.at[2])
    put_bas = pltpu.make_async_copy(basis_if, bas_all.at[me], ld.at[3])
    load_inv.start()
    put_idx.start()
    put_bas.start()
    load_schur.start()

    gi = Gather(na, nb, idx_all, isend, irecv)
    gb = Gather(na, nb, bas_all, bsend, brecv)
    gc = Gather(na, nb, con_all, csend, crecv)
    gs = Gather(na, nb, sol_all, ssend, srecv)
    gg = Gather(na, nb, gbuf, ass_, ars)

    barrier = pltpu.get_barrier_semaphore()
    a, b, c = gi.a, gi.b, gi.c
    links = (
        (a + 1 < na, gi.slot(a + 1, b, c)),
        (a >= 1, gi.slot(a - 1, b, c)),
        (b + 1 < nb, gi.slot(a, b + 1, c)),
        (b >= 1, gi.slot(a, b - 1, c)),
    )
    for cond, target in links:

        @pl.when(cond)
        def _(target=target):
            pl.semaphore_signal(barrier, inc=1, device_id=(node, target), device_id_type=MESH)

    pl.semaphore_signal(barrier, inc=1, device_id=(node, gi.slot(a, b, 1 - c)), device_id_type=MESH)
    for p in range(1, nodes):
        pl.semaphore_signal(
            barrier, inc=1, device_id=((node + p) % nodes, me), device_id_type=MESH
        )
    count = nodes
    for cond, _t in links:
        count = count + cond.astype(jnp.int32)
    pl.semaphore_wait(barrier, count)
    put_idx.wait()
    gi.step(0)
    put_bas.wait()
    gb.step(0)
    load_inv.wait()

    cr = 256
    per_part = ni // cr
    chunks = 2 * per_part
    y = basis_in[...]

    def solve_chunk(q, _):
        part = q // per_part
        r0 = pl.multiple_of((q % per_part) * cr, cr)
        out = jnp.dot(inv[part, pl.ds(r0, cr), :], y, preferred_element_type=F32)
        solve[part, pl.ds(r0, cr), :] = out.astype(BF16)
        return 0

    lax.fori_loop(0, chunks, solve_chunk, 0)
    for part in range(2):
        out = lax.dot_general(couple[...], solve[part], TN, preferred_element_type=F32)
        con_all[me, :, pl.ds(part * m, m)] = out.astype(BF16)
    gc.step(0)
    for tau in range(1, gi.steps):
        gi.step(tau)
    gi.finish()
    for tau in range(1, gb.steps):
        gb.step(tau)
        if tau < 2:
            gc.step(tau)

    load_schur.wait()
    s2 = schur[...].reshape(2 * lg, total)

    def perm_pair(q, _):
        iota = lax.broadcasted_iota(jnp.int32, (total, LANE), 0)
        hot = jnp.concatenate(
            [(iota == idx_all[2 * q + k]).astype(BF16) for k in range(2)], axis=1
        )
        got = jnp.dot(s2, hot, preferred_element_type=F32)
        sperm[q] = got.astype(BF16)
        return 0

    lax.fori_loop(0, subs // 2, perm_pair, 0)
    for tau in range(2, gc.steps):
        gc.step(tau)
    gb.finish()
    base = jnp.dot(s2, bas_all[...].reshape(total, m), preferred_element_type=F32)
    gc.finish()

    work[...] = jnp.zeros_like(work)

    @pl.loop(0, subs // 2)
    def _(q):
        rhs = con_all[pl.ds(2 * q, 2)].reshape(2 * lg, 2 * m)
        work[...] += jnp.dot(sperm[q], rhs, preferred_element_type=F32)

    sol_re = base[:lg] - work[:lg, :m] + work[lg:, m:]
    sol_im = base[lg:] - work[:lg, m:] - work[lg:, :m]
    sol_all[me, :, pl.ds(0, m)] = sol_re.astype(BF16)
    sol_all[me, :, pl.ds(m, m)] = sol_im.astype(BF16)
    gs.step(0)
    wr = weights[node * 0, 0]
    wi = weights[node * 0, 1]
    t_if = wr * sol_re.astype(BF16).astype(F32) - wi * sol_im.astype(BF16).astype(F32)
    term[pl.ds(ni, lg), :] = t_if
    tsend[pl.ds(ni, lg), :] = t_if.astype(BF16)
    rowid = jnp.broadcast_to(index[...], (LANE, LANE)).T
    for tau in range(1, gs.steps):
        gs.step(tau)
    gs.finish()

    lanes = lax.broadcasted_iota(jnp.int32, (LANE, LANE), 1)
    sel = jnp.concatenate(
        [(lanes + LANE * k == rowid).astype(BF16) for k in range(total // LANE)], axis=1
    )
    picked = jnp.dot(sel, sol_all[...].reshape(total, 2 * m), preferred_element_type=F32).astype(BF16)

    def pq_chunk(q, _):
        r0 = pl.multiple_of(q * cr, cr)
        cor = jnp.dot(couple[pl.ds(r0, cr), :], picked, preferred_element_type=F32)
        d_re = basis_in[pl.ds(r0, cr), :].astype(F32) - cor[:, :m]
        d_im = cor[:, m:]
        solve[0, pl.ds(r0, cr), :] = (wr * d_re + wi * d_im).astype(BF16)
        solve[1, pl.ds(r0, cr), :] = (wr * d_im - wi * d_re).astype(BF16)
        return 0

    lax.fori_loop(0, per_part, pq_chunk, 0)

    def term_chunk(q, _):
        r0 = pl.multiple_of(q * cr, cr)
        out = jnp.dot(inv[0, pl.ds(r0, cr), :], solve[0], preferred_element_type=F32)
        out += jnp.dot(inv[1, pl.ds(r0, cr), :], solve[1], preferred_element_type=F32)
        term[pl.ds(r0, cr), :] = out
        tsend[pl.ds(r0, cr), :] = out.astype(BF16)
        return 0

    lax.fori_loop(0, per_part, term_chunk, 0)

    def share(k):
        return pl.ds(pl.multiple_of(k * ch, 16), ch)

    def term_copy(p):
        peer = (node + p) % nodes
        return pltpu.make_async_remote_copy(
            src_ref=tsend.at[share(peer)], dst_ref=trecv.at[p - 1],
            send_sem=tss.at[p - 1], recv_sem=trs.at[p - 1],
            device_id=(peer, me), device_id_type=MESH,
        )

    def filt_copy(p):
        peer = (node + p) % nodes
        return pltpu.make_async_remote_copy(
            src_ref=filt.at[share(node)], dst_ref=filt.at[share(node)],
            send_sem=fss.at[p - 1], recv_sem=frs.at[p - 1],
            device_id=(peer, me), device_id_type=MESH,
        )

    for p in range(1, nodes):
        term_copy(p).start()
    for p in range(1, nodes):
        term_copy(p).wait()
    own = term[share(node), :]
    for p in range(1, nodes):
        own += trecv[p - 1].astype(F32)
    own = own.astype(BF16)
    filt[share(node), :] = own
    for p in range(1, nodes):
        filt_copy(p).start()

    nbk = m // LANE
    at = 0
    for rb in range(nbk):
        blk = lax.dot_general(
            own[:, rb * LANE : (rb + 1) * LANE], own[:, rb * LANE :], TN, preferred_element_type=F32
        )
        for k in range(nbk - rb):
            g6[pl.ds(at * LANE, LANE), :] = blk[:, k * LANE : (k + 1) * LANE]
            at += 1
    r6 = g6.shape[0] // subs

    def piece(k):
        return pl.ds(pl.multiple_of(k * r6, 8), r6)

    def gram_copy(p):
        peer = (me + p) % subs
        return pltpu.make_async_remote_copy(
            src_ref=g6.at[piece(peer)], dst_ref=grecv.at[me],
            send_sem=gss.at[p], recv_sem=grs.at[p],
            device_id=(node, peer), device_id_type=MESH,
        )

    @pl.loop(1, subs)
    def _(p):
        gram_copy(p).start()

    grecv[me] = g6[piece(me), :]

    @pl.loop(1, subs)
    def _(p):
        gram_copy(p).wait()

    part = grecv[0]
    for k in range(1, subs):
        part += grecv[k]
    nrecv[node] = part

    def node_copy(p):
        peer = (node + p) % nodes
        return pltpu.make_async_remote_copy(
            src_ref=nrecv.at[node], dst_ref=nrecv.at[node],
            send_sem=nss.at[p - 1], recv_sem=nrs.at[p - 1],
            device_id=(peer, me), device_id_type=MESH,
        )

    for p in range(1, nodes):
        node_copy(p).start()
    for p in range(1, nodes):
        node_copy(p).wait()
    full = nrecv[0]
    for k in range(1, nodes):
        full += nrecv[k]
    gbuf[me] = full
    for tau in range(gg.steps):
        gg.step(tau)
    gg.finish()
    for p in range(1, nodes):
        filt_copy(p).wait()


def factor_kernel(scale, g6, filt, out_inner, out_iface, tw, uall, wall):
    m = filt.shape[1]
    nbk = m // LANE
    width = LANE * (nbk + 1)
    row8 = lax.broadcasted_iota(jnp.int32, (8, LANE), 0)
    groups = LANE // 8
    hi = lax.Precision.HIGHEST
    at = 0
    for blk in range(nbk):
        nu = nbk - blk
        for k in range(nu):
            tw[:, k * LANE : (k + 1) * LANE] = g6[(at + k) * LANE : (at + k + 1) * LANE, :] * scale
        at += nu
        ri = lax.broadcasted_iota(jnp.int32, (LANE, LANE), 0)
        ci = lax.broadcasted_iota(jnp.int32, (LANE, LANE), 1)
        for k in range(blk + 1):
            tile = (ri == ci).astype(F32) if k == blk else jnp.zeros((LANE, LANE), F32)
            tw[:, (nu + k) * LANE : (nu + k + 1) * LANE] = tile
        for p in range(blk):
            left = uall[p, :, blk * LANE : (blk + 1) * LANE]
            tw[:, : nu * LANE] -= lax.dot_general(
                left, uall[p, :, blk * LANE :], TN, precision=hi, preferred_element_type=F32
            )
            tw[:, nu * LANE : (nu + p + 1) * LANE] -= lax.dot_general(
                left, wall[p, :, : (p + 1) * LANE], TN, precision=hi, preferred_element_type=F32
            )

        @pl.loop(0, groups)
        def _(p):
            r0 = pl.multiple_of(8 * p, 8)
            x = tw[pl.ds(r0, 8), :]
            d = x[:, :LANE]
            cols = [jnp.broadcast_to(d[:, j : j + 1], (8, LANE)) for j in range(8)]
            tiles = [x[:, k * LANE : (k + 1) * LANE] for k in range(nbk + 1)]
            inv, low, us = [], [], []
            diag = jnp.ones((8, LANE), F32)
            for j in range(8):
                piv = jnp.broadcast_to(cols[j][j : j + 1, :], (8, LANE))
                r = lax.rsqrt(piv)
                r = r * (1.5 - 0.5 * piv * r * r)
                inv.append(r)
                lj = cols[j] * r
                lows = {}
                for k in range(j + 1, 8):
                    lows[k] = jnp.broadcast_to(lj[k : k + 1, :], (8, LANE))
                    cols[k] = cols[k] - lj * lows[k]
                low.append(lows)
                diag = jnp.where(row8 == j, r, diag)
                lm = jnp.where(row8 > j, lj, 0.0)
                u = [jnp.broadcast_to(t[j : j + 1, :], (8, LANE)) * r for t in tiles]
                us.append(u)
                tiles = [t - lm * uu for t, uu in zip(tiles, u)]
            tiles = [t * diag for t in tiles]
            for g in range(groups):
                live = (g > p).astype(F32)
                xg = tw[8 * g : 8 * g + 8, :]
                tg = [xg[:, k * LANE : (k + 1) * LANE] for k in range(nbk + 1)]
                cg = [jnp.broadcast_to(tg[0][:, j : j + 1], (8, LANE)) for j in range(8)]
                for j in range(8):
                    lj = cg[j] * (inv[j] * live)
                    for k in range(j + 1, 8):
                        cg[k] = cg[k] - lj * low[j][k]
                    tg = [t - lj * uu for t, uu in zip(tg, us[j])]
                tg[0] = pltpu.roll(tg[0], LANE - 8, 1)
                for k in range(nbk + 1):
                    tw[8 * g : 8 * g + 8, k * LANE : (k + 1) * LANE] = tg[k]
            for k in range(1, nbk + 1):
                tw[pl.ds(r0, 8), k * LANE : (k + 1) * LANE] = tiles[k]

        if nu > 1:
            uall[blk, :, (blk + 1) * LANE :] = tw[:, LANE : nu * LANE]
        wall[blk, :, : (blk + 1) * LANE] = tw[:, nu * LANE :]
        if nu > 1:
            wall[blk, :, (blk + 1) * LANE :] = jnp.zeros((LANE, (nu - 1) * LANE), F32)

    w = wall[...].reshape(m, m)
    w_hi = w.astype(BF16)
    w_lo = (w - w_hi.astype(F32)).astype(BF16)

    def apply(rows):
        out = lax.dot_general(rows, w_hi, NT, preferred_element_type=F32)
        return out + lax.dot_general(rows, w_lo, NT, preferred_element_type=F32)

    ni = out_inner.shape[0]

    @pl.loop(0, ni // LANE)
    def _(q):
        r0 = pl.multiple_of(q * LANE, LANE)
        out_inner[pl.ds(r0, LANE), :] = apply(filt[pl.ds(r0, LANE), :])

    out_iface[...] = apply(filt[pl.ds(ni, LANE), :])


def per_device(
    inner_inverse, schur_inverse, coupling, iface_index, basis_inner, basis_iface, node_weights
):
    subs, nodes = lax.axis_size("sub"), lax.axis_size("node")
    na = 4
    nb = subs // (2 * na)
    ni, m = basis_inner.shape
    lg = basis_iface.shape[0]
    total = schur_inverse.shape[3]
    rows = ni + lg
    ch = rows // nodes
    nbk = m // LANE
    n6 = nbk * (nbk + 1) // 2 * LANE
    r6 = n6 // subs
    vm = pl.BlockSpec(memory_space=pltpu.VMEM)
    hbm = pl.BlockSpec(memory_space=pl.ANY)
    dma = pltpu.SemaphoreType.DMA

    def pair():
        return [dma((5, subs // 2)), dma((subs,))]

    peers = max(nodes - 1, 1)
    filt, gram = pl.pallas_call(
        functools.partial(step_kernel, (na, nb, nodes)),
        out_shape=(
            jax.ShapeDtypeStruct((rows, m), BF16),
            jax.ShapeDtypeStruct((subs, r6, LANE), F32),
        ),
        in_specs=[hbm, hbm, vm, vm, vm, vm, pl.BlockSpec(memory_space=pltpu.SMEM)],
        out_specs=(vm, vm),
        scratch_shapes=[
            pltpu.VMEM((2, ni, ni), BF16),
            pltpu.VMEM((2, lg, total), BF16),
            pltpu.VMEM((2, ni, m), BF16),
            pltpu.VMEM((subs, 1, lg), jnp.int32),
            pltpu.VMEM((subs, lg, m), BF16),
            pltpu.VMEM((subs, lg, 2 * m), BF16),
            pltpu.VMEM((subs, lg, 2 * m), BF16),
            pltpu.VMEM((subs // 2, 2 * lg, 2 * lg), BF16),
            pltpu.VMEM((2 * lg, 2 * m), F32),
            pltpu.VMEM((rows, m), F32),
            pltpu.VMEM((rows, m), BF16),
            pltpu.VMEM((peers, ch, m), BF16),
            pltpu.VMEM((n6, LANE), F32),
            pltpu.VMEM((subs, r6, LANE), F32),
            pltpu.VMEM((nodes, r6, LANE), F32),
            dma((4,)),
            *pair(), *pair(), *pair(), *pair(),
            dma((peers,)), dma((peers,)), dma((peers,)), dma((peers,)),
            dma((subs,)), dma((subs,)), dma((peers,)), dma((peers,)),
            *pair(),
        ],
        compiler_params=pltpu.CompilerParams(
            collective_id=0, has_side_effects=True, vmem_limit_bytes=60 * 1024 * 1024
        ),
    )(
        inner_inverse[0, 0], schur_inverse[0], coupling[0], iface_index, basis_inner, basis_iface,
        node_weights,
    )
    return pl.pallas_call(
        functools.partial(factor_kernel, 1.0 / (subs * rows)),
        out_shape=(
            jax.ShapeDtypeStruct((ni, m), F32),
            jax.ShapeDtypeStruct((lg, m), F32),
        ),
        in_specs=[vm, vm],
        out_specs=(vm, vm),
        scratch_shapes=[
            pltpu.VMEM((LANE, LANE * (nbk + 1)), F32),
            pltpu.VMEM((nbk, LANE, m), F32),
            pltpu.VMEM((nbk, LANE, m), F32),
        ],
        compiler_params=pltpu.CompilerParams(vmem_limit_bytes=40 * 1024 * 1024),
    )(gram.reshape(n6, LANE), filt)


def solution(mesh):
    return jax.shard_map(
        per_device,
        mesh=mesh,
        in_specs=(
            P("node", "sub", None, None, None),
            P("node", None, "sub", None),
            P("sub", None, None),
            P("sub", None),
            P("sub", None),
            P("sub", None),
            P("node", None),
        ),
        out_specs=(P("sub", None), P("sub", None)),
        check_vma=False,
    )
```

time: 463 us -> 155 us (0.33); the launches traced: 456 us -> 155 us
  waiting for transfers between devices: 229 us -> 0 us
  Pallas kernels: 0 us -> 152 us
  other arithmetic: 112 us -> 0 us
  matrix products: 38.7 us -> 0 us
  local copies, waits for them, and re-layouts: 36.2 us -> 2.16 us
  blocking collectives: 23.1 us -> 0 us
  between operations: 16.2 us -> 0.65 us
    pallas_call x0 -> x2, Pallas kernels: none -> 152 us  [the longest x1 123 us: per_device(): pl.pallas_call(functools.partial(step_kernel, (na, nb, nodes)), out_shape...]
    psum x2 -> x0, waiting for transfers between devices: 146 us -> none  [the longest x1 92.1 us: per_device(): gram_matrix = lax.psum(gram_part(filt_inner, filt_iface), 'sub')]
    another operation x17 -> x0, other arithmetic: 97.9 us -> none  [the longest x10 61.6 us: cholesky_apply(): lower_factor = jnp.linalg.cholesky(gram_matrix)]
    all_gather x3 -> x0, waiting for transfers between devices: 81.9 us -> none  [the longest x1 42.1 us: per_device(): block_piece = lax.all_gather(iface_solution, 'sub', axis=0, tiled=True)]
    dot_general x8 -> x0, matrix products: 25.1 us -> none  [the longest x1 8.7 us: per_device(): jnp.dot(stacked_inverse, correction, preferred_element_type=jnp.float32)]
    all_gather x1 -> x0, blocking collectives: 23.1 us -> none  [per_device(): lax.all_gather(iface_index, 'sub', axis=0, tiled=True)]
    another operation x14 -> x0, matrix products: 13.6 us -> none  [the longest x5 5.53 us: cholesky_apply(): lax.linalg.triangular_solve(lower_factor, second_rows, left_side=False, l...]
    gather x1 -> x0, local copies, waits for them, and re-layouts: 12.4 us -> none  [per_device(): arranged = jnp.take(all_contrib, inverse_order, axis=0).astype(jnp.float32)]
  transfers between devices with their start and end apart: 5 -> 0, of which waited for: 5 -> 0; matrix products, arithmetic and copies ran while one was open for 6% -> 0% of each run, Pallas kernels for 0% -> 0%
where the time goes in v1:
time: 155 us
  Pallas kernels  152 us (98%)
  local copies, waits for them, and re-layouts  2.16 us (1%)
    pallas_call x1, Pallas kernels, per_device(): pl.pallas_call(functools.partial(step_kernel, (na, nb, nodes)), out_shape...  123 us
    pallas_call x1, Pallas kernels, per_device(): pl.pallas_call(functools.partial(factor_kernel, 1.0 / (subs * rows)), out...  29 us

profile of v1, /device:TPU:0, one launch (start us, length us, event | category | flops | bytes accessed | tf_op | source)
XLA Modules:
  0.0 154.5 jit_solution(6351266370989560962)
XLA Ops:
  0.6 122.7 %shard_map.86 = (bf16[1152,384]{1,0:T(8,128)(2,1)}, f32[16,48,128]{2,1,0:T(8,128)}) custom-call(bf16[2,1024,1024]{2,1,0:T(8,128)(2,1)} %bitcast.5, bf16[2,128,2048]{2,1,0:T(8,128)(2,1)} %bitcast.6, bf16[1024,128]{1,0:T(8,128)(2,1)} %bitcast.7, s32[1,128]{1,0:T(1,128)} %index.1, bf16[1024,384]{1,0:T(8,128)(2,1)} %basis_in.1, bf16[128,384]{1,0:T(8,128)(2,1)} %basis_if.1, ...), custom_call_target="tpu_custom_call" | custom-call | tf_op jit(solution)/shard_map/pallas_call | solution.py:461
  123.3 0.0 copy-start
  123.4 1.2 copy-done
  124.5 0.0 copy-start.1
  124.5 1.0 copy-done.1
  125.5 29.0 %shard_map.87 = (f32[1024,384]{1,0:T(8,128)}, f32[128,384]{1,0:T(8,128)}) custom-call(f32[768,128]{1,0:T(8,128)S(1)} %bitcast.4, bf16[1152,384]{1,0:T(8,128)(2,1)S(1)} %copy-done), custom_call_target="tpu_custom_call" | custom-call | tf_op jit(solution)/shard_map/pallas_call | solution.py:498
Async XLA Ops:
  123.3 1.2 copy-start
  124.5 1.0 copy-start.1

commit v2 on v1

--- a/solution.py
+++ b/solution.py
@@ -101,7 +101,7 @@
 def step_kernel(
     dims, inv_hbm, schur_hbm, couple, index, basis_in, basis_if, weights,
     filt, gbuf,
-    inv, schur, solve, idx_all, bas_all, con_all, sol_all, sperm, work, term, tsend, trecv, g6, grecv, nrecv,
+    inv, schur, solve, uv, idx_all, bas_all, con_all, sol_all, bperm, sperm, work, term, tsend, trecv, g6, grecv, nrecv,
     ld, isend, irecv, bsend, brecv, csend, crecv, ssend, srecv, tss, trs, fss, frs, gss, grs, nss, nrs, ass_, ars,
 ):
     na, nb, nodes = dims
@@ -111,7 +111,6 @@
     lg = couple.shape[1]
     total = schur.shape[2]
     rows = ni + lg
-    ch = rows // nodes
     node = lax.axis_index("node")
     me = lax.axis_index("sub")
 
@@ -128,7 +127,6 @@
     gb = Gather(na, nb, bas_all, bsend, brecv)
     gc = Gather(na, nb, con_all, csend, crecv)
     gs = Gather(na, nb, sol_all, ssend, srecv)
-    gg = Gather(na, nb, gbuf, ass_, ars)
 
     barrier = pltpu.get_barrier_semaphore()
     a, b, c = gi.a, gi.b, gi.c
@@ -176,13 +174,15 @@
         out = lax.dot_general(couple[...], solve[part], TN, preferred_element_type=F32)
         con_all[me, :, pl.ds(part * m, m)] = out.astype(BF16)
     gc.step(0)
-    for tau in range(1, gi.steps):
+    last = gi.steps - 1
+    gi.step(1)
+    gb.step(1)
+    for tau in range(2, gi.steps):
         gi.step(tau)
+        gb.step(tau)
+        if tau < last:
+            gc.step(tau - 1)
     gi.finish()
-    for tau in range(1, gb.steps):
-        gb.step(tau)
-        if tau < 2:
-            gc.step(tau)
 
     load_schur.wait()
     s2 = schur[...].reshape(2 * lg, total)
@@ -197,91 +197,123 @@
         return 0
 
     lax.fori_loop(0, subs // 2, perm_pair, 0)
-    for tau in range(2, gc.steps):
-        gc.step(tau)
+    gc.step(last - 1)
     gb.finish()
-    base = jnp.dot(s2, bas_all[...].reshape(total, m), preferred_element_type=F32)
+
+    lanes = lax.broadcasted_iota(jnp.int32, (LANE, LANE), 1)
+
+    def selector(row):
+        rowid = jnp.broadcast_to(row, (LANE, LANE)).T
+        return jnp.concatenate(
+            [(lanes + LANE * k == rowid).astype(BF16) for k in range(total // LANE)], axis=1
+        )
+
+    def perm_rows(q, _):
+        got = jnp.dot(
+            selector(idx_all[q]), bas_all[...].reshape(total, m), preferred_element_type=F32
+        )
+        bperm[q] = got.astype(BF16)
+        return 0
+
+    lax.fori_loop(0, subs, perm_rows, 0)
+    gc.step(last)
     gc.finish()
 
     work[...] = jnp.zeros_like(work)
 
     @pl.loop(0, subs // 2)
     def _(q):
-        rhs = con_all[pl.ds(2 * q, 2)].reshape(2 * lg, 2 * m)
+        con = con_all[pl.ds(2 * q, 2)].reshape(2 * lg, 2 * m)
+        bas = bperm[pl.ds(2 * q, 2)].reshape(2 * lg, m)
+        rhs_re = (bas.astype(F32) - con[:, :m].astype(F32)).astype(BF16)
+        rhs = jnp.concatenate([rhs_re, -con[:, m:]], axis=1)
         work[...] += jnp.dot(sperm[q], rhs, preferred_element_type=F32)
 
-    sol_re = base[:lg] - work[:lg, :m] + work[lg:, m:]
-    sol_im = base[lg:] - work[:lg, m:] - work[lg:, :m]
+    sol_re = work[:lg, :m] - work[lg:, m:]
+    sol_im = work[:lg, m:] + work[lg:, :m]
     sol_all[me, :, pl.ds(0, m)] = sol_re.astype(BF16)
     sol_all[me, :, pl.ds(m, m)] = sol_im.astype(BF16)
     gs.step(0)
-    wr = weights[node * 0, 0]
-    wi = weights[node * 0, 1]
+    wr = weights[0, 0]
+    wi = weights[0, 1]
     t_if = wr * sol_re.astype(BF16).astype(F32) - wi * sol_im.astype(BF16).astype(F32)
     term[pl.ds(ni, lg), :] = t_if
     tsend[pl.ds(ni, lg), :] = t_if.astype(BF16)
-    rowid = jnp.broadcast_to(index[...], (LANE, LANE)).T
+    sh_in, sh_if = ni // nodes, lg // nodes
+    half = sh_in // 2
+
+    def piece_of(k, i):
+        if i == 2:
+            return pl.ds(pl.multiple_of(ni + k * sh_if, 16), sh_if), pl.ds(sh_in, sh_if)
+        return pl.ds(pl.multiple_of(k * sh_in + i * half, 16), half), pl.ds(i * half, half)
+
+    def term_copy(p, i):
+        peer = (node + p) % nodes
+        src, dst = piece_of(peer, i)
+        return pltpu.make_async_remote_copy(
+            src_ref=tsend.at[src], dst_ref=trecv.at[p - 1, dst],
+            send_sem=tss.at[p - 1, i], recv_sem=trs.at[p - 1, i],
+            device_id=(peer, me), device_id_type=MESH,
+        )
+
+    def filt_copy(p, i):
+        peer = (node + p) % nodes
+        src, _ = piece_of(node, i)
+        return pltpu.make_async_remote_copy(
+            src_ref=filt.at[src], dst_ref=filt.at[src],
+            send_sem=fss.at[p - 1, i], recv_sem=frs.at[p - 1, i],
+            device_id=(peer, me), device_id_type=MESH,
+        )
+
+    for p in range(1, nodes):
+        term_copy(p, 2).start()
+    sel = selector(index[...])
     for tau in range(1, gs.steps):
         gs.step(tau)
     gs.finish()
 
-    lanes = lax.broadcasted_iota(jnp.int32, (LANE, LANE), 1)
-    sel = jnp.concatenate(
-        [(lanes + LANE * k == rowid).astype(BF16) for k in range(total // LANE)], axis=1
-    )
     picked = jnp.dot(sel, sol_all[...].reshape(total, 2 * m), preferred_element_type=F32).astype(BF16)
 
-    def pq_chunk(q, _):
+    def uv_chunk(q, _):
         r0 = pl.multiple_of(q * cr, cr)
         cor = jnp.dot(couple[pl.ds(r0, cr), :], picked, preferred_element_type=F32)
-        d_re = basis_in[pl.ds(r0, cr), :].astype(F32) - cor[:, :m]
-        d_im = cor[:, m:]
-        solve[0, pl.ds(r0, cr), :] = (wr * d_re + wi * d_im).astype(BF16)
-        solve[1, pl.ds(r0, cr), :] = (wr * d_im - wi * d_re).astype(BF16)
+        cor = cor.astype(BF16).astype(F32)
+        uv[0, pl.ds(r0, cr), :] = (wr * cor[:, :m] - wi * cor[:, m:]).astype(BF16)
+        uv[1, pl.ds(r0, cr), :] = -(wi * cor[:, :m] + wr * cor[:, m:]).astype(BF16)
         return 0
 
-    lax.fori_loop(0, per_part, pq_chunk, 0)
-
-    def term_chunk(q, _):
-        r0 = pl.multiple_of(q * cr, cr)
-        out = jnp.dot(inv[0, pl.ds(r0, cr), :], solve[0], preferred_element_type=F32)
-        out += jnp.dot(inv[1, pl.ds(r0, cr), :], solve[1], preferred_element_type=F32)
-        term[pl.ds(r0, cr), :] = out
-        tsend[pl.ds(r0, cr), :] = out.astype(BF16)
-        return 0
-
-    lax.fori_loop(0, per_part, term_chunk, 0)
-
-    def share(k):
-        return pl.ds(pl.multiple_of(k * ch, 16), ch)
-
-    def term_copy(p):
-        peer = (node + p) % nodes
-        return pltpu.make_async_remote_copy(
-            src_ref=tsend.at[share(peer)], dst_ref=trecv.at[p - 1],
-            send_sem=tss.at[p - 1], recv_sem=trs.at[p - 1],
-            device_id=(peer, me), device_id_type=MESH,
-        )
-
-    def filt_copy(p):
-        peer = (node + p) % nodes
-        return pltpu.make_async_remote_copy(
-            src_ref=filt.at[share(node)], dst_ref=filt.at[share(node)],
-            send_sem=fss.at[p - 1], recv_sem=frs.at[p - 1],
-            device_id=(peer, me), device_id_type=MESH,
-        )
+    lax.fori_loop(0, per_part, uv_chunk, 0)
+
+    def term_piece(k, i):
+        r, _ = piece_of(k, i)
+        out = jnp.dot(inv[0, r, :], uv[0], preferred_element_type=F32)
+        out += jnp.dot(inv[1, r, :], uv[1], preferred_element_type=F32)
+        z_re = solve[0, r, :].astype(F32)
+        z_im = solve[1, r, :].astype(F32)
+        return wr * z_re - wi * z_im - out
 
     for p in range(1, nodes):
-        term_copy(p).start()
-    for p in range(1, nodes):
-        term_copy(p).wait()
-    own = term[share(node), :]
-    for p in range(1, nodes):
-        own += trecv[p - 1].astype(F32)
-    own = own.astype(BF16)
-    filt[share(node), :] = own
-    for p in range(1, nodes):
-        filt_copy(p).start()
+        for i in range(2):
+            r, _ = piece_of((node + p) % nodes, i)
+            tsend[r, :] = term_piece((node + p) % nodes, i).astype(BF16)
+            term_copy(p, i).start()
+    for i in range(2):
+        r, _ = piece_of(node, i)
+        term[r, :] = term_piece(node, i)
+    own = []
+    for i in (2, 0, 1):
+        r, d = piece_of(node, i)
+        for p in range(1, nodes):
+            term_copy(p, i).wait()
+        got = term[r, :]
+        for p in range(1, nodes):
+            got += trecv[p - 1, d, :].astype(F32)
+        got = got.astype(BF16)
+        filt[r, :] = got
+        for p in range(1, nodes):
+            filt_copy(p, i).start()
+        own.append(got)
+    own = jnp.concatenate([own[1], own[2], own[0]], axis=0)
 
     nbk = m // LANE
     at = 0
@@ -336,14 +368,60 @@
     for k in range(1, nodes):
         full += nrecv[k]
     gbuf[me] = full
-    for tau in range(gg.steps):
-        gg.step(tau)
-    gg.finish()
+
+    places = subs // 2
+    spot = me // 2
+    sibling = me + 1 - 2 * c
+
+    def plane_copy(p):
+        return pltpu.make_async_remote_copy(
+            src_ref=gbuf.at[me], dst_ref=gbuf.at[me],
+            send_sem=ass_.at[0, p], recv_sem=ars.at[me],
+            device_id=(node, ((spot + p) % places) * 2 + c), device_id_type=MESH,
+        )
+
+    def from_plane(p):
+        origin = ((spot + places - p) % places) * 2 + c
+        return pltpu.make_async_remote_copy(
+            src_ref=gbuf.at[origin], dst_ref=gbuf.at[origin],
+            send_sem=ass_.at[1, p], recv_sem=ars.at[origin],
+            device_id=(node, sibling), device_id_type=MESH,
+        )
+
+    def from_sibling(p):
+        origin = p * 2 + 1 - c
+        return pltpu.make_async_remote_copy(
+            src_ref=gbuf.at[origin], dst_ref=gbuf.at[origin],
+            send_sem=ass_.at[1, 0], recv_sem=ars.at[origin],
+            device_id=(node, sibling), device_id_type=MESH,
+        )
+
+    @pl.loop(1, places)
+    def _(p):
+        plane_copy(p).start()
+
+    from_plane(0).start()
+
+    @pl.loop(1, places)
+    def _(p):
+        from_plane(p).wait_recv()
+        from_plane(p).start()
+
+    @pl.loop(0, places)
+    def _(p):
+        from_sibling(p).wait_recv()
+        from_plane(p).wait_send()
+
+    @pl.loop(1, places)
+    def _(p):
+        plane_copy(p).wait_send()
+
     for p in range(1, nodes):
-        filt_copy(p).wait()
-
-
-def factor_kernel(scale, g6, filt, out_inner, out_iface, tw, uall, wall):
+        for i in range(3):
+            filt_copy(p, i).wait()
+
+
+def factor_kernel(scale, g6, filt, out_inner, out_iface, tw, urow, held, uall, wall):
     m = filt.shape[1]
     nbk = m // LANE
     width = LANE * (nbk + 1)
@@ -370,13 +448,23 @@
                 left, wall[p, :, : (p + 1) * LANE], TN, precision=hi, preferred_element_type=F32
             )
 
-        @pl.loop(0, groups)
-        def _(p):
-            r0 = pl.multiple_of(8 * p, 8)
-            x = tw[pl.ds(r0, 8), :]
-            d = x[:, :LANE]
-            cols = [jnp.broadcast_to(d[:, j : j + 1], (8, LANE)) for j in range(8)]
-            tiles = [x[:, k * LANE : (k + 1) * LANE] for k in range(nbk + 1)]
+        nt = nbk + 1
+
+        def split(v):
+            return [v[:, k * LANE : (k + 1) * LANE] for k in range(nt)]
+
+        def update(tg, fac, live):
+            inv, low, us = fac
+            cg = [jnp.broadcast_to(tg[0][:, j : j + 1], (8, LANE)) for j in range(8)]
+            for j in range(8):
+                lj = cg[j] * inv[j] if live is None else cg[j] * (inv[j] * live)
+                for k in range(j + 1, 8):
+                    cg[k] = cg[k] - lj * low[j][k]
+                tg = [t - lj * uu for t, uu in zip(tg, us[j])]
+            return [pltpu.roll(tg[0], LANE - 8, 1)] + tg[1:]
+
+        def factor(tiles):
+            cols = [jnp.broadcast_to(tiles[0][:, j : j + 1], (8, LANE)) for j in range(8)]
             inv, low, us = [], [], []
             diag = jnp.ones((8, LANE), F32)
             for j in range(8):
@@ -395,26 +483,50 @@
                 u = [jnp.broadcast_to(t[j : j + 1, :], (8, LANE)) * r for t in tiles]
                 us.append(u)
                 tiles = [t - lm * uu for t, uu in zip(tiles, u)]
-            tiles = [t * diag for t in tiles]
-            for g in range(groups):
-                live = (g > p).astype(F32)
-                xg = tw[8 * g : 8 * g + 8, :]
-                tg = [xg[:, k * LANE : (k + 1) * LANE] for k in range(nbk + 1)]
-                cg = [jnp.broadcast_to(tg[0][:, j : j + 1], (8, LANE)) for j in range(8)]
-                for j in range(8):
-                    lj = cg[j] * (inv[j] * live)
-                    for k in range(j + 1, 8):
-                        cg[k] = cg[k] - lj * low[j][k]
-                    tg = [t - lj * uu for t, uu in zip(tg, us[j])]
-                tg[0] = pltpu.roll(tg[0], LANE - 8, 1)
-                for k in range(nbk + 1):
+            return (inv, low, us), [t * diag for t in tiles]
+
+        def keep(fac):
+            inv, low, us = fac
+            at = 0
+            for j in range(8):
+                for v in [inv[j]] + [low[j][k] for k in range(j + 1, 8)] + us[j]:
+                    held[at] = v
+                    at += 1
+
+        def kept():
+            at, inv, low, us = 0, [], [], []
+            for j in range(8):
+                inv.append(held[at])
+                low.append({k: held[at + k - j] for k in range(j + 1, 8)})
+                us.append([held[at + 8 - j + k] for k in range(nt)])
+                at += 8 - j + nt
+            return inv, low, us
+
+        def put(r0, tiles):
+            for k in range(1, nt):
+                urow[pl.ds(r0, 8), k * LANE : (k + 1) * LANE] = tiles[k]
+
+        first, rows0 = factor(split(tw[pl.ds(0, 8), :]))
+        keep(first)
+        put(0, rows0)
+
+        @pl.loop(0, groups - 1)
+        def _(p):
+            r1 = pl.multiple_of(8 * p + 8, 8)
+            fac = kept()
+            ahead = update(split(tw[pl.ds(r1, 8), :]), fac, None)
+            groups_now = [tw[8 * g : 8 * g + 8, :] for g in range(1, groups)]
+            nxt, done = factor(ahead)
+            for g in range(1, groups):
+                tg = update(split(groups_now[g - 1]), fac, (g > p).astype(F32))
+                for k in range(nt):
                     tw[8 * g : 8 * g + 8, k * LANE : (k + 1) * LANE] = tg[k]
-            for k in range(1, nbk + 1):
-                tw[pl.ds(r0, 8), k * LANE : (k + 1) * LANE] = tiles[k]
+            keep(nxt)
+            put(r1, done)
 
         if nu > 1:
-            uall[blk, :, (blk + 1) * LANE :] = tw[:, LANE : nu * LANE]
-        wall[blk, :, : (blk + 1) * LANE] = tw[:, nu * LANE :]
+            uall[blk, :, (blk + 1) * LANE :] = urow[:, LANE : nu * LANE]
+        wall[blk, :, : (blk + 1) * LANE] = urow[:, nu * LANE :]
         if nu > 1:
             wall[blk, :, (blk + 1) * LANE :] = jnp.zeros((LANE, (nu - 1) * LANE), F32)
 
@@ -470,10 +582,12 @@
             pltpu.VMEM((2, ni, ni), BF16),
             pltpu.VMEM((2, lg, total), BF16),
             pltpu.VMEM((2, ni, m), BF16),
+            pltpu.VMEM((2, ni, m), BF16),
             pltpu.VMEM((subs, 1, lg), jnp.int32),
             pltpu.VMEM((subs, lg, m), BF16),
             pltpu.VMEM((subs, lg, 2 * m), BF16),
             pltpu.VMEM((subs, lg, 2 * m), BF16),
+            pltpu.VMEM((subs, lg, m), BF16),
             pltpu.VMEM((subs // 2, 2 * lg, 2 * lg), BF16),
             pltpu.VMEM((2 * lg, 2 * m), F32),
             pltpu.VMEM((rows, m), F32),
@@ -484,7 +598,7 @@
             pltpu.VMEM((nodes, r6, LANE), F32),
             dma((4,)),
             *pair(), *pair(), *pair(), *pair(),
-            dma((peers,)), dma((peers,)), dma((peers,)), dma((peers,)),
+            dma((peers, 3)), dma((peers, 3)), dma((peers, 3)), dma((peers, 3)),
             dma((subs,)), dma((subs,)), dma((peers,)), dma((peers,)),
             *pair(),
         ],
@@ -505,6 +619,8 @@
         out_specs=(vm, vm),
         scratch_shapes=[
             pltpu.VMEM((LANE, LANE * (nbk + 1)), F32),
+            pltpu.VMEM((LANE, LANE * (nbk + 1)), F32),
+            pltpu.VMEM((36 + 8 * (nbk + 1), 8, LANE), F32),
             pltpu.VMEM((nbk, LANE, m), F32),
             pltpu.VMEM((nbk, LANE, m), F32),
         ],

time: 155 us -> 145 us (0.935)
  Pallas kernels: 152 us -> 142 us
    pallas_call x1, Pallas kernels: 123 us -> 103 us  [per_device(): pl.pallas_call(functools.partial(step_kernel, (na, nb, nodes)), out_shape...]
    pallas_call x1, Pallas kernels: 29 us -> 39.2 us  [per_device(): pl.pallas_call(functools.partial(factor_kernel, 1.0 / (subs * rows)), out...]
where the time goes in v2:
time: 145 us
  Pallas kernels  142 us (98%)
  local copies, waits for them, and re-layouts  2.16 us (1%)
    pallas_call x1, Pallas kernels, per_device(): pl.pallas_call(functools.partial(step_kernel, (na, nb, nodes)), out_shape...  103 us
    pallas_call x1, Pallas kernels, per_device(): pl.pallas_call(functools.partial(factor_kernel, 1.0 / (subs * rows)), out...  39.2 us

profile of v2, /device:TPU:0, one launch (start us, length us, event | category | flops | bytes accessed | tf_op | source)
XLA Modules:
  0.0 145.2 jit_solution(6255088347764910165)
XLA Ops:
  0.6 103.1 %shard_map.86 = (bf16[1152,384]{1,0:T(8,128)(2,1)}, f32[16,48,128]{2,1,0:T(8,128)}) custom-call(bf16[2,1024,1024]{2,1,0:T(8,128)(2,1)} %bitcast.5, bf16[2,128,2048]{2,1,0:T(8,128)(2,1)} %bitcast.6, bf16[1024,128]{1,0:T(8,128)(2,1)} %bitcast.7, s32[1,128]{1,0:T(1,128)} %index.1, bf16[1024,384]{1,0:T(8,128)(2,1)} %basis_in.1, bf16[128,384]{1,0:T(8,128)(2,1)} %basis_if.1, ...), custom_call_target="tpu_custom_call" | custom-call | tf_op jit(solution)/shard_map/pallas_call | solution.py:573
  103.8 0.0 copy-start
  103.8 1.2 copy-done
  104.9 0.0 copy-start.1
  104.9 1.0 copy-done.1
  105.9 39.2 %shard_map.87 = (f32[1024,384]{1,0:T(8,128)}, f32[128,384]{1,0:T(8,128)}) custom-call(f32[768,128]{1,0:T(8,128)S(1)} %bitcast.4, bf16[1152,384]{1,0:T(8,128)(2,1)S(1)} %copy-done), custom_call_target="tpu_custom_call" | custom-call | tf_op jit(solution)/shard_map/pallas_call | solution.py:612
Async XLA Ops:
  103.8 1.2 copy-start
  104.9 1.0 copy-start.1
